TPU v7x, 128 devices: a whole 4x4x4 slice. The times are simulated.
128 devices in a mesh: req: 4 (over y), seq: 32 (over x, z, core).
Axes of the slice: x: 4, y: 4, z: 4, core: 2. Of those that a mesh axis runs over, the one named last changes fastest.
Arguments:
- query: bfloat16 [8, 2048, 2048], P('req', 'seq')
- fresh_kv: bfloat16 [8, 2048, 2048], P('req', 'seq'), may hold values from -6 to 6
- residual: bfloat16 [8, 2048, 2304], P('req', 'seq')
- kv_cache: bfloat16 [8, 64, 16, 2048], P('req', 'seq'), may hold values from -6 to 6
- page_table: int32 [8, 32, 2], P('req', 'seq'), may hold values from 0 to 1, each once within a row
- cache_length: int32 [8], replicated, may hold values from 256 to 1024, as said below
- slot_request: int32 [8], replicated, may hold values from 0 to 7, each once
- w_out: bfloat16 [2048, 2304], P('req'), may hold values from -0.125 to 0.125
- w_gate: bfloat16 [2304, 4608], P(None, 'req'), may hold values from -0.125 to 0.125
- w_up: bfloat16 [2304, 4608], P(None, 'req'), may hold values from -0.125 to 0.125
- w_down: bfloat16 [4608, 2304], P('req'), may hold values from -0.09375 to 0.09375
- gain_attn: float32 [2304], replicated, may hold values from 0.1 to 1.9
- gain_pre: float32 [2304], replicated, may hold values from 0.1 to 1.9
- gain_post: float32 [2304], replicated, may hold values from 0.1 to 1.9
Outputs:
- output: bfloat16 [8, 2048, 2304], P('req', 'seq')
Inputs may be any that keep to these rules, and one draw needn't show every extreme that they name: `slot_request`: each request has exactly one slot. `page_table`: each row of 2 entries names each of 0 to 1 once. `cache_length`: some request has exactly 1024 cached positions and some exactly 256.
All inputs are finite; a program needn't handle non-finite values.
Results may differ from a plain program's by a relative error of at most 0.015.
Values may be sent and summed in bfloat16 or wider, within the bound.
A program may use at most 192 MiB of HBM per device.

v0:
```python
import jax
import jax.numpy as jnp
from jax import lax
from jax.sharding import PartitionSpec as P

H = 8
KV = 4
HD = 256


SOFT_CAP = 50.0
EPSILON = 1e-06


def rms_scale(tensor, scale_gain):
    return (
        tensor * lax.rsqrt(jnp.mean(tensor * tensor, axis=-1, keepdims=True) + EPSILON) * scale_gain
    )


def score_block(grouped, portion, allowed):
    kv_width = portion.shape[-1] // 2
    key_rows = portion[..., :kv_width].reshape(portion.shape[0], portion.shape[1], KV, HD)
    value_rows = portion[..., kv_width:].reshape(portion.shape[0], portion.shape[1], KV, HD)
    scores = jnp.einsum(
        "rnkgd,rmkd->rkgnm", grouped, key_rows, preferred_element_type=jnp.float32
    ) * HD ** (-0.5)
    capped = SOFT_CAP * jnp.tanh(scores / SOFT_CAP)
    weights = jnp.where(allowed[:, None, None], jnp.exp(capped), 0.0).astype(jnp.bfloat16)
    denominator = jnp.sum(weights, axis=-1, dtype=jnp.float32)
    summed = jnp.einsum(
        "rkgnm,rmkd->rnkgd", weights, value_rows, preferred_element_type=jnp.float32
    )
    return (summed, denominator)


def body(
    query,
    fresh_kv,
    residual,
    kv_cache,
    page_table,
    cache_length,
    slot_request,
    w_out,
    w_gate,
    w_up,
    w_down,
    gain_attn,
    gain_pre,
    gain_post,
):
    req_dev, row_count = (query.shape[0], query.shape[1])
    pages_dev, page_len, pair_width = (kv_cache.shape[1], kv_cache.shape[2], kv_cache.shape[3])
    span_cache = pages_dev * page_len
    groups = lax.axis_size("req")
    my_group = lax.axis_index("req")
    my_seq = lax.axis_index("seq")
    pick_page = (page_table[:, 0, :, None] == jnp.arange(pages_dev)[None, None, :]).astype(
        jnp.bfloat16
    )
    ordered = jnp.einsum("rlp,rpsw->rlsw", pick_page, kv_cache, preferred_element_type=jnp.float32)
    ordered = ordered.astype(jnp.bfloat16).reshape(req_dev, span_cache, pair_width)
    holder = slot_request // req_dev
    within = slot_request % req_dev
    sending = (holder == my_group)[:, None] & (within[:, None] == jnp.arange(req_dev)[None, :])
    outgoing = jnp.einsum(
        "sj,jlw->slw", sending.astype(jnp.bfloat16), ordered, preferred_element_type=jnp.float32
    ).astype(jnp.bfloat16)
    arrived = lax.all_to_all(outgoing, "req", split_axis=0, concat_axis=0, tiled=True)
    arrived = arrived.reshape(groups, req_dev, span_cache, pair_width)
    mine_req = lax.dynamic_slice_in_dim(slot_request, my_group * req_dev, req_dev)
    source = mine_req // req_dev
    choose = source[None, :] == jnp.arange(groups)[:, None]
    cache_here = jnp.sum(
        jnp.where(choose[:, :, None, None], arrived, jnp.zeros((), jnp.bfloat16)), axis=0
    )
    match_req = mine_req[:, None] == jnp.arange(slot_request.shape[0])[None, :]
    my_len = jnp.sum(jnp.where(match_req, cache_length[None, :], 0), axis=1)
    grouped = query.reshape(req_dev, row_count, KV, H // KV, HD)
    row_pos = my_seq * row_count + jnp.arange(row_count)
    joined = jnp.concatenate([cache_here, fresh_kv], axis=1)
    span_all = span_cache + row_count
    portion = lax.all_gather(joined, "seq", axis=1, tiled=True)
    position_all = jnp.arange(portion.shape[1])
    holder_dev = position_all // span_all
    offset = position_all % span_all
    in_cache = offset < span_cache
    allowed = jnp.where(
        in_cache[None, None, :],
        ((holder_dev * span_cache + offset)[None, :] < my_len[:, None])[:, None, :],
        ((holder_dev * row_count + offset - span_cache)[None, :] <= row_pos[:, None])[None],
    )
    summed, denominator = score_block(grouped, portion, allowed)
    running = (summed, denominator)
    summed, denominator = running
    attended = (
        (summed / jnp.moveaxis(denominator, 3, 1)[..., None])
        .astype(jnp.bfloat16)
        .reshape(req_dev, row_count, -1)
    )
    partial_out = jnp.einsum(
        "srk,kd->srd",
        lax.all_to_all(attended, "req", split_axis=2, concat_axis=0, tiled=True),
        w_out,
        preferred_element_type=jnp.float32,
    )
    slot_here = (jnp.arange(groups) == my_group)[:, None, None, None]
    placed = jnp.where(slot_here, residual.astype(jnp.float32)[None], 0.0).reshape(
        groups * req_dev, row_count, residual.shape[2]
    )
    full_out, every_resid = (
        lax.psum(partial_out.astype(jnp.bfloat16), "req").astype(jnp.float32),
        lax.psum(placed.astype(jnp.bfloat16), "req").astype(jnp.float32),
    )
    layer_state = every_resid + rms_scale(full_out, gain_attn)
    portion = rms_scale(layer_state, gain_pre).astype(jnp.bfloat16)
    gate_proj = jnp.einsum("srd,df->srf", portion, w_gate, preferred_element_type=jnp.float32)
    up_proj = jnp.einsum("srd,df->srf", portion, w_up, preferred_element_type=jnp.float32)
    hidden = (jax.nn.gelu(gate_proj, approximate=True) * up_proj).astype(jnp.bfloat16)
    own_state = lax.dynamic_slice_in_dim(layer_state, my_group * req_dev, req_dev, 0)
    mlp_out = lax.psum_scatter(
        jnp.einsum("srf,fd->srd", hidden, w_down, preferred_element_type=jnp.float32).astype(
            jnp.bfloat16
        ),
        "req",
        scatter_dimension=0,
        tiled=True,
    ).astype(jnp.float32)
    return (own_state + rms_scale(mlp_out, gain_post)).astype(jnp.bfloat16)


def solution(mesh):
    in_specs = (
        P("req", "seq", None),
        P("req", "seq", None),
        P("req", "seq", None),
        P("req", "seq", None, None),
        P("req", "seq", None),
        P(),
        P(),
        P("req", None),
        P(None, "req"),
        P(None, "req"),
        P("req", None),
        P(),
        P(),
        P(),
    )
    out_specs = P("req", "seq", None)
    return jax.shard_map(body, mesh=mesh, in_specs=in_specs, out_specs=out_specs, check_vma=False)
```

profile of v0, /device:TPU:1, one launch (start us, length us, event | category | flops | bytes accessed | tf_op | source)
XLA Modules:
  0.0 417.4 jit_solution(1069927505175992656)
XLA Ops:
  6.5 0.8 and_select_fusion
  7.4 0.7 fusion.55
  8.0 1.5 convolution_convert_fusion.2
  9.5 0.1 copy.42
  9.6 0.5 convolution_convert_fusion.1
  10.1 1.6 copy.44
  11.7 5.0 %all-to-all-start = ((bf16[8,32,2048]{2,1,0:T(8,128)(2,1)}), bf16[8,32,2048]{2,1,0:T(8,128)(2,1)S(1)}, u32[]{:S(2)}, u32[]{:S(2)}) async-start(bf16[8,32,2048]{2,1,0:T(8,128)(2,1)} %copy.44), calls=%async_computation | async-start | bytes 2097152 | tf_op jit(solution)/shard_map/all_to_all | solution.py:70
  16.7 2.4 copy.46
  19.1 0.1 and_select_fusion.2
  19.2 11.8 %all-to-all-done = bf16[8,32,2048]{2,1,0:T(8,128)(2,1)S(1)} async-done(((bf16[8,32,2048]{2,1,0:T(8,128)(2,1)}), bf16[8,32,2048]{2,1,0:T(8,128)(2,1)S(1)}, u32[]{:S(2)}, u32[]{:S(2)}) %all-to-all-start) | async-done | bytes 1048608 | tf_op jit(solution)/shard_map/all_to_all | solution.py:70
  30.9 1.3 fusion.36
  32.2 3.0 pad_maximum_fusion
  35.2 0.0 all-gather.2.cloned.1.call-update
  35.3 1.4 reshape.170
  36.8 0.2 fusion.50
  37.0 0.1 broadcast_compare_fusion.1
  37.1 0.2 broadcast_compare_fusion
  37.2 0.2 broadcast_select_fusion.1
  37.4 91.9 %all-gather.2.cloned.1.call-done = bf16[2,3072,2048]{2,0,1:T(2,128)(2,1)} async-done(((bf16[2,96,2048]{2,0,1:T(2,128)(2,1)}), bf16[2,3072,2048]{2,0,1:T(2,128)(2,1)}) %all-gather.2.cloned.1.call-update) | async-done | bytes 25165840 | tf_op jit(solution)/shard_map/all_gather | solution.py:84
  129.3 20.1 %fusion.57 = (bf16[2,3072,1024]{2,0,1:T(2,128)(2,1)}, bf16[2,3072,1024]{2,0,1:T(2,128)(2,1)}) fusion(bf16[2,3072,2048]{2,0,1:T(2,128)(2,1)} %all-gather.2.cloned.1.call-done), kind=kLoop, calls=%fused_computation.91 | loop fusion | bytes 50331648 | tf_op jit(solution)/shard_map/slice | solution.py:23
  149.4 31.3 %copy.67 = bf16[2,3072,1024]{1,2,0:T(8,128)(2,1)} copy(bf16[2,3072,1024]{2,0,1:T(2,128)(2,1)} %get-tuple-element.11) | data formatting | bytes 25165824
  180.7 31.2 %copy.66 = bf16[2,3072,1024]{1,2,0:T(8,128)(2,1)} copy(bf16[2,3072,1024]{2,0,1:T(2,128)(2,1)} %get-tuple-element.12) | data formatting | bytes 25165824
  211.9 9.6 %convert_reduce_fusion = (f32[2,4,2,64]{3,2,1,0:T(2,128)S(1)}, bf16[2,4,2,64,3072]{4,3,2,1,0:T(8,128)(2,1)}) fusion(bf16[2,3072,4,256,1]{1,3,4,2,0:T(8,128)(2,1)} %bitcast.67, bf16[2,64,4,2,256]{4,3,2,1,0:T(2,128)(2,1)S(1)} %reshape.170, pred[2,64,3072]{2,1,0:T(8,128)(4,1)S(1)} %broadcast_select_fusion.1), kind=kOutput, calls=%fused_computation.2 | convolution fusion | flops 1629486080 | bytes 19795968 | tf_op jit(solution)/shard_map/rnkgd,rmkd->rkgnm/dot_general | solution.py:25
  221.4 11.5 %fusion.31 = bf16[2,64,4,2,256]{4,1,3,2,0:T(8,128)(2,1)} fusion(bf16[2,3072,4,256,1]{1,3,4,2,0:T(8,128)(2,1)} %bitcast.68, bf16[2,4,2,64,3072]{4,3,2,1,0:T(8,128)(2,1)} %get-tuple-element.14, f32[2,64,4,2]{1,3,2,0:T(2,128)S(1)} %bitcast.82), kind=kOutput, calls=%fused_computation.38 | convolution fusion | flops 1611137024 | bytes 19402752 | tf_op jit(solution)/shard_map/rkgnm,rmkd->rnkgd/dot_general | solution.py:31
  232.9 2.4 copy.63
  235.3 1.6 reshape.180
  236.8 4.1 all-to-all-start.1
  241.0 0.2 all-reduce.3.cloned.1.call-start
  241.2 0.1 broadcast_in_dim.113
  241.3 0.1 broadcast_in_dim.114
  241.4 2.9 fusion.10
  244.2 5.9 %all-to-all-done.1 = bf16[4,2,32768]{2,1,0:T(2,128)(2,1)} async-done(((bf16[4,2,32768]{2,1,0:T(2,128)(2,1)}), bf16[4,2,32768]{2,1,0:T(2,128)(2,1)}, u32[]{:S(2)}, u32[]{:S(2)}) %all-to-all-start.1) | async-done | bytes 524320 | tf_op jit(solution)/shard_map/all_to_all | solution.py:104
  250.2 1.7 reshape.181
  251.9 1.9 copy.64
  253.8 1.1 copy.55
  254.9 2.9 convolution_convert_fusion
  257.8 0.0 all-reduce.3.cloned.1.call-update
  257.8 0.0 reduce-scatter.2.cloned.1.call-start
  257.9 99.4 %all-reduce.3.cloned.1.call-done = (bf16[8,64,2304]{2,1,0:T(8,128)(2,1)}, bf16[8,64,2304]{2,1,0:T(8,128)(2,1)}) async-done(((bf16[8,64,2304]{2,1,0:T(8,128)(2,1)}, bf16[8,64,2304]{2,1,0:T(8,128)(2,1)}), (bf16[8,64,2304]{2,1,0:T(8,128)(2,1)}, bf16[8,64,2304]{2,1,0:T(8,128)(2,1)})) %all-reduce.3.cloned.1.call-update) | async-done | bytes 4718608 | tf_op jit(solution)/shard_map/psum | solution.py:113
  357.3 2.3 fusion.7
  359.7 3.7 multiply_reduce_fusion
  363.5 3.6 fusion.26
  367.1 3.4 fusion.17
  370.6 4.5 %fusion.11 = bf16[8,64,2304]{2,1,0:T(8,128)(2,1)} fusion(bf16[8,64,1152]{2,1,0:T(8,128)(2,1)S(1)} %fusion.17, bf16[1152,2304]{1,0:T(8,128)(2,1)S(1)} %bitcast.80), kind=kOutput, calls=%fused_computation.18 | convolution fusion | flops 2719088640 | bytes 8847360 | tf_op jit(solution)/shard_map/srf,fd->srd/dot_general | solution.py:123
  375.1 0.0 reduce-scatter.2.cloned.1.call-update
  375.1 32.0 %reduce-scatter.2.cloned.1.call-done = bf16[2,64,2304]{2,1,0:T(8,128)(2,1)} async-done(((bf16[8,64,2304]{2,1,0:T(8,128)(2,1)}), bf16[2,64,2304]{2,1,0:T(8,128)(2,1)}) %reduce-scatter.2.cloned.1.call-update) | async-done | bytes 589840 | tf_op jit(solution)/shard_map/reduce_scatter | solution.py:122
  407.1 1.3 fusion.32
  408.3 2.5 fusion.35
  (39 shorter events, 0.2 us)
Async XLA Ops:
  6.5 248.4 %copy-start = (bf16[512,2304]{1,0:T(8,128)(2,1)S(1)}, bf16[512,2304]{1,0:T(8,128)(2,1)}, u32[]{:S(2)}) copy-start(bf16[512,2304]{1,0:T(8,128)(2,1)} %param.21) | copy-start | bytes 7077892
  6.5 12.5 %copy-start.4 = (s32[8]{0:T(128)S(1)}, s32[8]{0:T(128)}, u32[]{:S(2)}) copy-start(s32[8]{0:T(128)} %param.20) | copy-start | bytes 100
  10.1 26.7 %copy-start.6 = (s32[8]{0:T(128)S(1)}, s32[8]{0:T(128)}, u32[]{:S(2)}) copy-start(s32[8]{0:T(128)} %param.19) | copy-start | bytes 100
  11.7 19.2 %all-to-all-start = ((bf16[8,32,2048]{2,1,0:T(8,128)(2,1)}), bf16[8,32,2048]{2,1,0:T(8,128)(2,1)S(1)}, u32[]{:S(2)}, u32[]{:S(2)}) async-start(bf16[8,32,2048]{2,1,0:T(8,128)(2,1)} %copy.44), calls=%async_computation | async-start | bytes 2097152 | tf_op jit(solution)/shard_map/all_to_all | solution.py:70
  16.7 112.7 %all-gather.2.cloned.1.call-start = ((), (), s32[]{:S(2)}) async-start(), calls=%async_computation.3 | async-start | bytes 25952256 | tf_op jit(solution)/shard_map/all_gather | solution.py:84
  236.8 13.3 %all-to-all-start.1 = ((bf16[4,2,32768]{2,1,0:T(2,128)(2,1)}), bf16[4,2,32768]{2,1,0:T(2,128)(2,1)}, u32[]{:S(2)}, u32[]{:S(2)}) async-start(bf16[4,2,32768]{2,1,0:T(2,128)(2,1)} %reshape.180), calls=%async_computation.1 | async-start | bytes 1048576 | tf_op jit(solution)/shard_map/all_to_all | solution.py:104
  241.0 116.3 %all-reduce.3.cloned.1.call-start = ((), (), s32[]{:S(2)}) async-start(), calls=%async_computation.5 | async-start | bytes 9437184 | tf_op jit(solution)/shard_map/psum | solution.py:113
  257.8 101.8 %copy-start.2 = (f32[2304]{0:T(1024)S(1)}, f32[2304]{0:T(1024)}, u32[]{:S(2)}) copy-start(f32[2304]{0:T(1024)} %param.25) | copy-start | bytes 27652
  257.8 149.2 %reduce-scatter.2.cloned.1.call-start = ((), (), s32[]{:S(2)}) async-start(), calls=%async_computation.4 | async-start | bytes 2949120 | tf_op jit(solution)/shard_map/reduce_scatter | solution.py:122
  357.3 6.2 %slice-start = ((s8[5308416]{0:T(1024)(128)(4,1)}), s8[4194304]{0:T(1024)(128)(4,1)S(1)}, s32[]{:S(2)}) async-start(s8[5308416]{0:T(1024)(128)(4,1)} %bitcast.75), calls=%async_computation.6 | async-start | bytes 8388608
  357.3 6.2 %copy-start.5 = (f32[2304]{0:T(1024)S(1)}, f32[2304]{0:T(1024)}, u32[]{:S(2)}) copy-start(f32[2304]{0:T(1024)} %param.26) | copy-start | bytes 27652
  359.6 3.8 slice-start.1
  359.6 7.5 %slice-start.2 = ((s8[5308416]{0:T(1024)(128)(4,1)}), s8[4194304]{0:T(1024)(128)(4,1)S(1)}, s32[]{:S(2)}) async-start(s8[5308416]{0:T(1024)(128)(4,1)} %bitcast.77), calls=%async_computation.8 | async-start | bytes 8388608
  359.6 10.9 %slice-start.4 = ((s8[5308416]{0:T(1024)(128)(4,1)}), s8[4194304]{0:T(1024)(128)(4,1)S(1)}, s32[]{:S(2)}) async-start(s8[5308416]{0:T(1024)(128)(4,1)} %bitcast.79), calls=%async_computation.10 | async-start | bytes 8388608
  363.4 3.7 copy-start.1
  363.5 3.7 slice-start.3
  363.5 7.1 %slice-start.5 = ((s8[5308416]{0:T(1024)(128)(4,1)}), s8[1114112]{0:T(1024)(128)(4,1)S(1)}, s32[]{:S(2)}) async-start(s8[5308416]{0:T(1024)(128)(4,1)} %bitcast.79), calls=%async_computation.11 | async-start | bytes 2228224
  370.5 37.8 %copy-start.3 = (f32[2304]{0:T(1024)S(1)}, f32[2304]{0:T(1024)}, u32[]{:S(2)}) copy-start(f32[2304]{0:T(1024)} %param.27) | copy-start | bytes 27652
Sparse Core Ops, SparseCore 0:
  35.4 93.9 all-gather.1
  258.0 99.2 all-reduce.2
  375.2 31.8 reduce-scatter.1
where the time goes:
time: 420 us; the launch traced here: 417 us
  waiting for transfers between devices  241 us (57%)
  local copies, waits for them, and re-layouts  96.9 us (23%)
  matrix products  37.4 us (9%)
  other arithmetic  19.3 us (5%)
  between operations  13.4 us (3%)
  starting transfers between devices  9.4 us (2%)
    psum x1, waiting for transfers between devices, body(): lax.psum(partial_out.astype(jnp.bfloat16), 'req').astype(jnp.float32)  99.4 us
    all_gather x1, waiting for transfers between devices, body(): portion = lax.all_gather(joined, 'seq', axis=1, tiled=True)  91.9 us
    unnamed x31, local copies, waits for them, and re-layouts  68.2 us
    reduce_scatter x1, waiting for transfers between devices, body(): lax.psum_scatter(jnp.einsum('srf,fd->srd', hidden, w_down, preferred_elem...  32 us
    slice x1, local copies, waits for them, and re-layouts, score_block(): portion[..., :kv_width].reshape(portion.shape[0], portion.shape[1], KV, HD)  20.1 us
    all_to_all x1, waiting for transfers between devices, body(): lax.all_to_all(outgoing, 'req', split_axis=0, concat_axis=0, tiled=True)  11.8 us
    dot_general x1, matrix products, score_block(): jnp.einsum('rkgnm,rmkd->rnkgd', weights, value_rows, preferred_element_ty...  11.5 us
    dot_general x1, matrix products, score_block(): jnp.einsum('rnkgd,rmkd->rkgnm', grouped, key_rows, preferred_element_type...  9.55 us
  transfers between devices with their start and end apart: 5, of which 5 were waited for; matrix products, arithmetic and copies ran while one was open for 2% of the time, Pallas kernels for 0%

commit v1 on v0

v1 whole, which is shorter than its diff:
```python
import jax
import jax.numpy as jnp
from jax import lax
from jax.experimental import pallas as pl
from jax.experimental.pallas import tpu as pltpu
from jax.sharding import PartitionSpec as P

H = 8
KV = 4
HD = 256
SOFT_CAP = 50.0
EPSILON = 1e-06
LOG2E = 1.4426950408889634
MESH = pl.DeviceIdType.MESH


def rms_scale(tensor, scale_gain):
    return (
        tensor * lax.rsqrt(jnp.mean(tensor * tensor, axis=-1, keepdims=True) + EPSILON) * scale_gain
    )


def attention_kernel(
    slot_ref,
    len_ref,
    q_ref,
    f_ref,
    c_ref,
    att_ref,
    qbuf,
    kvf,
    kvc,
    stage,
    order,
    obuf,
    acc,
    den,
    ca_send,
    ca_recv,
    q_send,
    q_recv,
    f_send,
    f_recv,
    cb_send,
    c_recv,
    fw_send,
    fd_recv,
    r_send,
    r_recv,
):
    y = lax.axis_index("req")
    s = lax.axis_index("seq")
    core = s % 2
    half = (s // 2) % 2
    slot = s // 4
    quarter = s % 4
    sibling = s + 1 - 2 * core

    def remote(src, dst, send, recv, to):
        return pltpu.make_async_remote_copy(
            src_ref=src, dst_ref=dst, send_sem=send, recv_sem=recv, device_id=to, device_id_type=MESH
        )

    def lanes(start):
        return pl.ds(pl.multiple_of(start, 256), 256)

    def cache_part(k, h):
        return c_ref.at[:, :, lanes(h * 1024 + k * 256)]

    def stage_part(owner, h):
        return stage.at[pl.ds(2 * owner, 2), :, pl.ds(h * 256, 256)]

    for d in range(1, 4):
        k = (y + d) % 4
        for h in range(2):
            remote(
                cache_part(k, h), stage_part(y, h), ca_send.at[d, h], ca_recv.at[y, h], (k, s)
            ).start()
    for h in range(2):
        pltpu.make_async_copy(cache_part(y, h), stage_part(y, h), ca_recv.at[y, h]).start()

    def fresh_copies(k, j, p, act):
        target = 4 * (2 * y + j) + 2 * p + core
        own = (k == y) & (target == s)
        n = (k * 2 + j) * 2 + p
        for h in range(2):
            src = f_ref.at[j, :, lanes(h * 1024 + k * 256)]
            dst = kvf.at[s, :, pl.ds(h * 256, 256)]

            @pl.when(jnp.logical_not(own))
            def _():
                cp = remote(src, dst, f_send.at[n, h], fd_recv.at[s, h], (k, target))
                if act == "start":
                    cp.start()
                else:
                    cp.wait_send()

            if act == "start":

                @pl.when(own)
                def _():
                    pltpu.make_async_copy(src, dst, fd_recv.at[s, h]).start()

    def query_copies(k, j, act):
        target = 4 * (2 * y + j) + quarter
        own = (k == y) & (target == s)
        n = k * 2 + j
        src = q_ref.at[j, :, pl.ds(pl.multiple_of(k * 512, 512), 512)]
        dst = qbuf.at[s // 4]

        @pl.when(jnp.logical_not(own))
        def _():
            cp = remote(src, dst, q_send.at[n], q_recv.at[s // 4], (k, target))
            if act == "start":
                cp.start()
            else:
                cp.wait_send()

        if act == "start":

            @pl.when(own)
            def _():
                pltpu.make_async_copy(src, dst, q_recv.at[s // 4]).start()

    def new_rows(act):
        for d in range(4):
            k = (y + d) % 4
            for j in range(2):
                for p in range(2):
                    fresh_copies(k, j, p, act)
        for d in range(4):
            k = (y + d) % 4
            for j in range(2):
                query_copies(k, j, act)

    new_rows("start")

    for owner in range(4):
        for h in range(2):
            pltpu.make_async_copy(stage_part(owner, h), stage_part(owner, h), ca_recv.at[owner, h]).wait()
    for i in range(8):
        order[i] = stage[slot_ref[i]]

    def cache_copies(i, p, act):
        target = 4 * i + 2 * p + core
        own = target == s
        src = order.at[i]
        dst = kvc.at[s]

        @pl.when(jnp.logical_not(own))
        def _():
            cp = remote(src, dst, cb_send.at[i, p], c_recv.at[s], (y, target))
            if act == "start":
                cp.start()
            else:
                cp.wait_send()

        if act == "start":

            @pl.when(own)
            def _():
                pltpu.make_async_copy(src, dst, c_recv.at[s]).start()

    for i in range(8):
        for p in range(2):
            cache_copies(i, p, "start")

    for j in range(16):
        src = 2 * j + core
        for h in range(2):
            part = kvf.at[src, :, pl.ds(h * 256, 256)]
            pltpu.make_async_copy(part, part, fd_recv.at[src, h]).wait()
        remote(kvf.at[src], kvf.at[src], fw_send.at[j, 0], f_recv.at[j], (y, sibling)).start()
    for j in range(16):
        src = 2 * j + core
        pltpu.make_async_copy(kvc.at[src], kvc.at[src], c_recv.at[src]).wait()
        remote(kvc.at[src], kvc.at[src], fw_send.at[j, 1], c_recv.at[src], (y, sibling)).start()
    for j in range(8):
        pltpu.make_async_copy(qbuf.at[j], qbuf.at[j], q_recv.at[j]).wait()
    for j in range(16):
        src = 2 * j + 1 - core
        pltpu.make_async_copy(kvf.at[src], kvf.at[src], f_recv.at[j]).wait()
        pltpu.make_async_copy(kvc.at[src], kvc.at[src], c_recv.at[src]).wait()

    length = len_ref[0]
    for n in range(12):
        fresh = n - 4
        if n < 4:
            keys = kvc[8 * n : 8 * n + 8].reshape(256, 512)
            first = 0
        else:
            keys = kvf[4 * fresh : 4 * fresh + 4].reshape(256, 512)
            first = fresh
        rows = 512 - 64 * first
        for g in range(2):
            queries = qbuf[first:, :, g * 256 : (g + 1) * 256].reshape(rows, 256)
            scores = lax.dot_general(
                queries, keys[:, :256], (((1,), (1,)), ((), ())), preferred_element_type=jnp.float32
            )
            weights = jnp.exp2(
                jnp.tanh(scores * (HD**-0.5 / SOFT_CAP)) * (SOFT_CAP * LOG2E)
            )
            if 0 < n < 4:
                lane = lax.broadcasted_iota(jnp.int32, (rows, 256), 1)
                weights = jnp.where(lane + 256 * n < length, weights, 0.0)
            if n >= 4:
                lane = lax.broadcasted_iota(jnp.int32, (64, 256), 1)
                line = lax.broadcasted_iota(jnp.int32, (64, 256), 0)
                edge = jnp.where(lane <= quarter * 64 + line, weights[:64], 0.0)
                weights = jnp.concatenate([edge, weights[64:]], axis=0) if rows > 64 else edge
            rounded = weights.astype(jnp.bfloat16)
            wide = rounded.astype(jnp.float32)
            total = wide[:, :128] + wide[:, 128:]
            summed = jnp.dot(rounded, keys[:, 256:], preferred_element_type=jnp.float32)
            if n == 0:
                acc[g] = summed
                den[g] = total
            else:
                acc[g, 64 * first :, :] += summed
                den[g, 64 * first :, :] += total
    for g in range(2):
        bottom = jnp.sum(den[g], axis=-1, keepdims=True)
        obuf[:, :, g * 256 : (g + 1) * 256] = (
            (acc[g] / bottom).astype(jnp.bfloat16).reshape(8, 64, 256)
        )

    def result_copies(j, act):
        target = quarter + 4 * j
        own = target == s
        src = obuf.at[j]
        dst = att_ref.at[slot]

        @pl.when(jnp.logical_not(own))
        def _():
            cp = remote(src, dst, r_send.at[j], r_recv.at[slot], (y, target))
            if act == "start":
                cp.start()
            else:
                cp.wait_send()

        if act == "start":

            @pl.when(own)
            def _():
                pltpu.make_async_copy(src, dst, r_recv.at[slot]).start()

    for j in range(8):
        result_copies(j, "start")
    for i in range(8):
        pltpu.make_async_copy(att_ref.at[i], att_ref.at[i], r_recv.at[i]).wait()

    for d in range(1, 4):
        k = (y + d) % 4
        for h in range(2):
            remote(
                cache_part(k, h), stage_part(y, h), ca_send.at[d, h], ca_recv.at[y, h], (k, s)
            ).wait_send()
    new_rows("wait")
    for i in range(8):
        for p in range(2):
            cache_copies(i, p, "wait")
    for j in range(16):
        src = 2 * j + core
        remote(kvf.at[src], kvf.at[src], fw_send.at[j, 0], f_recv.at[j], (y, sibling)).wait_send()
        remote(kvc.at[src], kvc.at[src], fw_send.at[j, 1], c_recv.at[src], (y, sibling)).wait_send()
    for j in range(8):
        result_copies(j, "wait")


def attention(slot_request, length, query, fresh, cache):
    dma = pltpu.SemaphoreType.DMA
    return pl.pallas_call(
        attention_kernel,
        out_shape=jax.ShapeDtypeStruct((8, 64, 512), jnp.bfloat16),
        in_specs=[
            pl.BlockSpec(memory_space=pltpu.SMEM),
            pl.BlockSpec(memory_space=pltpu.SMEM),
            pl.BlockSpec(memory_space=pltpu.VMEM),
            pl.BlockSpec(memory_space=pltpu.VMEM),
            pl.BlockSpec(memory_space=pltpu.VMEM),
        ],
        out_specs=pl.BlockSpec(memory_space=pltpu.VMEM),
        scratch_shapes=[
            pltpu.VMEM((8, 64, 512), jnp.bfloat16),
            pltpu.VMEM((32, 64, 512), jnp.bfloat16),
            pltpu.VMEM((32, 32, 512), jnp.bfloat16),
            pltpu.VMEM((8, 32, 512), jnp.bfloat16),
            pltpu.VMEM((8, 32, 512), jnp.bfloat16),
            pltpu.VMEM((8, 64, 512), jnp.bfloat16),
            pltpu.VMEM((2, 512, 256), jnp.float32),
            pltpu.VMEM((2, 512, 128), jnp.float32),
            dma((4, 2)),
            dma((4, 2)),
            dma((8,)),
            dma((8,)),
            dma((16, 2)),
            dma((16,)),
            dma((8, 2)),
            dma((32,)),
            dma((16, 2)),
            dma((32, 2)),
            dma((8,)),
            dma((8,)),
        ],
        compiler_params=pltpu.CompilerParams(
            has_side_effects=True, vmem_limit_bytes=40 * 1024 * 1024
        ),
        name="attention",
    )(slot_request, length, query, fresh, cache)


def body(
    query,
    fresh_kv,
    residual,
    kv_cache,
    page_table,
    cache_length,
    slot_request,
    w_out,
    w_gate,
    w_up,
    w_down,
    gain_attn,
    gain_pre,
    gain_post,
):
    req_dev, row_count = (query.shape[0], query.shape[1])
    pages_dev, page_len, pair_width = kv_cache.shape[1:]
    my_seq = lax.axis_index("seq")
    ordered = jnp.where(
        (page_table[:, 0, :] == 1)[:, :, None, None], kv_cache[:, 1:2], kv_cache[:, 0:1]
    ).reshape(req_dev, pages_dev * page_len, pair_width)
    my_request = lax.dynamic_slice_in_dim(slot_request, my_seq // 4, 1)
    my_len = jnp.sum(
        jnp.where(my_request == jnp.arange(cache_length.shape[0]), cache_length, 0)
    ).reshape(1)
    attended = attention(slot_request, my_len, query, fresh_kv, ordered)
    partial_out = jnp.einsum("srk,kd->srd", attended, w_out, preferred_element_type=jnp.float32)
    mixed = lax.psum_scatter(
        partial_out.astype(jnp.bfloat16), "req", scatter_dimension=0, tiled=True
    ).astype(jnp.float32)
    layer_state = residual.astype(jnp.float32) + rms_scale(mixed, gain_attn)
    normed = rms_scale(layer_state, gain_pre).astype(jnp.bfloat16)
    portion = lax.all_gather(normed, "req", axis=0, tiled=True)
    gate_proj = jnp.einsum("srd,df->srf", portion, w_gate, preferred_element_type=jnp.float32)
    up_proj = jnp.einsum("srd,df->srf", portion, w_up, preferred_element_type=jnp.float32)
    hidden = (jax.nn.gelu(gate_proj, approximate=True) * up_proj).astype(jnp.bfloat16)
    mlp_out = lax.psum_scatter(
        jnp.einsum("srf,fd->srd", hidden, w_down, preferred_element_type=jnp.float32).astype(
            jnp.bfloat16
        ),
        "req",
        scatter_dimension=0,
        tiled=True,
    ).astype(jnp.float32)
    return (layer_state + rms_scale(mlp_out, gain_post)).astype(jnp.bfloat16)


def solution(mesh):
    in_specs = (
        P("req", "seq", None),
        P("req", "seq", None),
        P("req", "seq", None),
        P("req", "seq", None, None),
        P("req", "seq", None),
        P(),
        P(),
        P("req", None),
        P(None, "req"),
        P(None, "req"),
        P("req", None),
        P(),
        P(),
        P(),
    )
    out_specs = P("req", "seq", None)
    return jax.shard_map(body, mesh=mesh, in_specs=in_specs, out_specs=out_specs, check_vma=False)
```

time: 420 us -> 258 us (0.61)
  waiting for transfers between devices: 241 us -> 99.1 us
  Pallas kernels: 0 us -> 105 us
  local copies, waits for them, and re-layouts: 96.9 us -> 5.16 us
  matrix products: 37.4 us -> 22.4 us
  starting transfers between devices: 9.4 us -> 0.27 us
  other arithmetic: 19.3 us -> 11.6 us
    pallas_call x0 -> x1, Pallas kernels: none -> 105 us  [attention(): pl.pallas_call(attention_kernel, out_shape=jax.ShapeDtypeStruct((8, 64, 5...]
    psum x1 -> x0, waiting for transfers between devices: 99.4 us -> none  [body(): lax.psum(partial_out.astype(jnp.bfloat16), 'req').astype(jnp.float32)]
    unnamed x31 -> x19, local copies, waits for them, and re-layouts: 68.2 us -> 2.76 us
    all_gather x1, waiting for transfers between devices: 91.9 us -> 32.5 us  [body(): portion = lax.all_gather(normed, 'req', axis=0, tiled=True)]
    reduce_scatter x0 -> x1, waiting for transfers between devices: none -> 34.5 us  [body(): lax.psum_scatter(partial_out.astype(jnp.bfloat16), 'req', scatter_dimensi...]
    dot_general x5 -> x1, matrix products: 25.9 us -> 2.81 us  [body(): jnp.einsum('srk,kd->srd', attended, w_out, preferred_element_type=jnp.flo...]
    slice x1 -> x0, local copies, waits for them, and re-layouts: 20.1 us -> none  [score_block(): portion[..., :kv_width].reshape(portion.shape[0], portion.shape[1], KV, HD)]
    all_to_all x2 -> x0, waiting for transfers between devices: 17.7 us -> none  [the longest x1 11.8 us: body(): lax.all_to_all(outgoing, 'req', split_axis=0, concat_axis=0, tiled=True)]
  transfers between devices with their start and end apart: 5 -> 3, of which waited for: 5 -> 3; matrix products, arithmetic and copies ran while one was open for 2% -> 0% of each run, Pallas kernels for 0% -> 0%
where the time goes in v1:
time: 258 us; the launch traced here: 257 us
  Pallas kernels  105 us (41%)
  waiting for transfers between devices  99.1 us (38%)
  matrix products  22.4 us (9%)
  between operations  13.2 us (5%)
  other arithmetic  11.6 us (4%)
  local copies, waits for them, and re-layouts  5.16 us (2%)
    pallas_call x1, Pallas kernels, attention(): pl.pallas_call(attention_kernel, out_shape=jax.ShapeDtypeStruct((8, 64, 5...  105 us
    reduce_scatter x1, waiting for transfers between devices, body(): lax.psum_scatter(partial_out.astype(jnp.bfloat16), 'req', scatter_dimensi...  34.5 us
    all_gather x1, waiting for transfers between devices, body(): portion = lax.all_gather(normed, 'req', axis=0, tiled=True)  32.5 us
    reduce_scatter x1, waiting for transfers between devices, body(): lax.psum_scatter(jnp.einsum('srf,fd->srd', hidden, w_down, preferred_elem...  32.2 us
    dot_general x1, matrix products, body(): jnp.einsum('srf,fd->srd', hidden, w_down, preferred_element_type=jnp.floa...  7.07 us
    dot_general x1, matrix products, body(): jnp.einsum('srd,df->srf', portion, w_gate, preferred_element_type=jnp.flo...  6.8 us
    dot_general x1, matrix products, body(): jnp.einsum('srd,df->srf', portion, w_up, preferred_element_type=jnp.float32)  5.76 us
  transfers between devices with their start and end apart: 3, of which 3 were waited for; matrix products, arithmetic and copies ran while one was open for 0% of the time, Pallas kernels for 0%

profile of v1, /device:TPU:1, one launch (start us, length us, event | category | flops | bytes accessed | tf_op | source)
XLA Modules:
  0.0 257.2 jit_solution(1953016997184181660)
XLA Ops:
  6.5 0.0 copy-start
  6.5 0.0 reduce-scatter.3.cloned.1.call-start
  6.5 0.8 broadcast_compare_fusion
  7.4 0.1 broadcast_in_dim.48
  7.5 0.1 broadcast_in_dim.49
  7.5 1.0 slice_bitcast_fusion.1
  8.5 1.2 dynamic_slice.3
  9.8 2.0 fusion.32
  11.7 0.1 bitcast_select_fusion.c_ref
  11.8 0.0 copy-start.1
  11.9 1.0 copy-done.1
  12.9 0.0 copy-start.2
  12.9 1.0 copy-done.2
  13.9 0.0 copy-start.3
  13.9 0.7 copy-done.3
  14.6 105.4 %attention.1 = bf16[8,64,512]{2,1,0:T(8,128)(2,1)S(1)} custom-call(s32[8]{0:T(128)S(1)} %copy-done.3, s32[1]{0:T(128)} %bitcast.1.len_ref, bf16[2,64,2048]{2,1,0:T(8,128)(2,1)S(1)} %copy-done.1, bf16[2,64,2048]{2,1,0:T(8,128)(2,1)S(1)} %copy-done.2, bf16[2,32,2048]{2,1,0:T(8,128)(2,1)S(1)} %bitcast_select_fusion.c_ref), custom_call_target="tpu_custom_call" | custom-call | tf_op jit(solution)/shard_map/attention/pallas_call | solution.py:272
  120.0 0.0 copy-done
  120.0 2.8 %convolution_convert_fusion = bf16[8,64,2304]{2,1,0:T(8,128)(2,1)} fusion(bf16[8,64,512]{2,1,0:T(8,128)(2,1)S(1)} %attention.1, bf16[512,2304]{1,0:T(8,128)(2,1)S(1)} %copy-done), kind=kOutput, calls=%fused_computation.7 | convolution fusion | flops 1209139200 | bytes 5242880 | tf_op jit(solution)/shard_map/srk,kd->srd/dot_general | solution.py:339
  122.9 0.0 copy-start.5
  122.9 0.0 copy-start.6
  122.9 0.0 copy-start.7
  122.9 0.0 reduce-scatter.3.cloned.1.call-update
  122.9 0.0 all-gather.2.cloned.1.call-start
  122.9 34.5 %reduce-scatter.3.cloned.1.call-done = bf16[2,64,2304]{2,1,0:T(8,128)(2,1)} async-done(((bf16[8,64,2304]{2,1,0:T(8,128)(2,1)}), bf16[2,64,2304]{2,1,0:T(8,128)(2,1)}) %reduce-scatter.3.cloned.1.call-update) | async-done | bytes 589840 | tf_op jit(solution)/shard_map/reduce_scatter | solution.py:340
  157.4 1.3 fusion.25
  158.7 0.0 copy-done.5
  158.7 0.0 copy-done.6
  158.7 1.5 multiply_reduce_fusion
  160.2 0.0 copy-done.7
  160.2 2.3 multiply_convert_fusion
  162.4 0.0 all-gather.2.cloned.1.call-update
  162.5 0.2 reduce-scatter.5.cloned.1.call-start
  162.7 32.5 %all-gather.2.cloned.1.call-done = bf16[8,64,2304]{2,1,0:T(8,128)(2,1)} async-done(((bf16[2,64,2304]{2,1,0:T(8,128)(2,1)}), bf16[8,64,2304]{2,1,0:T(8,128)(2,1)}) %all-gather.2.cloned.1.call-update) | async-done | bytes 2359312 | tf_op jit(solution)/shard_map/all_gather | solution.py:345
  195.2 0.0 copy-start.8
  195.2 6.8 %fusion.21 = f32[8,64,1152]{2,1,0:T(8,128)S(1)} fusion(bf16[8,64,2304]{2,1,0:T(8,128)(2,1)} %all-gather.2.cloned.1.call-done, bf16[2304,1152]{1,0:T(8,128)(2,1)} %param.22), kind=kOutput, calls=%fused_computation.17 | convolution fusion | flops 2722627584 | bytes 10027008 | tf_op jit(solution)/shard_map/srd,df->srf/dot_general | solution.py:346
  202.0 0.0 copy-done.8
  202.0 5.8 %fusion.12 = bf16[8,64,1152]{2,1,0:T(8,128)(2,1)S(1)} fusion(f32[8,64,1152]{2,1,0:T(8,128)S(1)} %fusion.21, bf16[8,64,2304]{2,1,0:T(8,128)(2,1)S(1)} %copy-done.8, bf16[2304,1152]{1,0:T(8,128)(2,1)} %param.23), kind=kOutput, calls=%fused_computation.10 | convolution fusion | flops 2719088640 | bytes 11206656 | tf_op jit(solution)/shard_map/srd,df->srf/dot_general | solution.py:347
  207.8 7.1 %fusion.6 = bf16[8,64,2304]{2,1,0:T(8,128)(2,1)} fusion(bf16[8,64,1152]{2,1,0:T(8,128)(2,1)S(1)} %fusion.12, bf16[1152,2304]{1,0:T(8,128)(2,1)} %param.24), kind=kOutput, calls=%fused_computation.6 | convolution fusion | flops 2719088640 | bytes 8847360 | tf_op jit(solution)/shard_map/srf,fd->srd/dot_general | solution.py:350
  214.8 0.0 copy-start.4
  214.8 0.0 reduce-scatter.5.cloned.1.call-update
  214.9 32.2 %reduce-scatter.5.cloned.1.call-done = bf16[2,64,2304]{2,1,0:T(8,128)(2,1)} async-done(((bf16[8,64,2304]{2,1,0:T(8,128)(2,1)}), bf16[2,64,2304]{2,1,0:T(8,128)(2,1)}) %reduce-scatter.5.cloned.1.call-update) | async-done | bytes 589840 | tf_op jit(solution)/shard_map/reduce_scatter | solution.py:349
  247.0 1.3 fusion.28
  248.3 0.0 copy-done.4
  248.3 2.4 fusion.31
  (4 shorter events, 0.0 us)
Async XLA Ops:
  6.5 113.5 %copy-start = (bf16[512,2304]{1,0:T(8,128)(2,1)S(1)}, bf16[512,2304]{1,0:T(8,128)(2,1)}, u32[]{:S(2)}) copy-start(bf16[512,2304]{1,0:T(8,128)(2,1)} %param.21) | copy-start | bytes 7077892
  6.5 150.9 %reduce-scatter.3.cloned.1.call-start = ((), (), s32[]{:S(2)}) async-start(), calls=%async_computation.2 | async-start | bytes 2949120 | tf_op jit(solution)/shard_map/reduce_scatter | solution.py:340
  11.8 1.0 copy-start.1
  12.9 1.0 copy-start.2
  13.9 0.7 copy-start.3
  122.9 35.8 %copy-start.5 = (bf16[2,64,2304]{2,1,0:T(8,128)(2,1)S(1)}, bf16[2,64,2304]{2,1,0:T(8,128)(2,1)}, u32[]{:S(2)}) copy-start(bf16[2,64,2304]{2,1,0:T(8,128)(2,1)} %param.16) | copy-start | bytes 1769476
  122.9 35.8 %copy-start.6 = (f32[2304]{0:T(1024)S(1)}, f32[2304]{0:T(1024)}, u32[]{:S(2)}) copy-start(f32[2304]{0:T(1024)} %param.25) | copy-start | bytes 27652
  122.9 37.3 %copy-start.7 = (f32[2304]{0:T(1024)S(1)}, f32[2304]{0:T(1024)}, u32[]{:S(2)}) copy-start(f32[2304]{0:T(1024)} %param.26) | copy-start | bytes 27652
  122.9 72.3 %all-gather.2.cloned.1.call-start = ((), (), s32[]{:S(2)}) async-start(), calls=%async_computation.3 | async-start | bytes 2949120 | tf_op jit(solution)/shard_map/all_gather | solution.py:345
  162.5 84.5 %reduce-scatter.5.cloned.1.call-start = ((), (), s32[]{:S(2)}) async-start(), calls=%async_computation.4 | async-start | bytes 2949120 | tf_op jit(solution)/shard_map/reduce_scatter | solution.py:349
  195.2 6.8 %copy-start.8 = (bf16[8,64,2304]{2,1,0:T(8,128)(2,1)S(1)}, bf16[8,64,2304]{2,1,0:T(8,128)(2,1)}, u32[]{:S(2)}) copy-start(bf16[8,64,2304]{2,1,0:T(8,128)(2,1)} %all-gather.2.cloned.1.call-done) | copy-start | bytes 7077892
  214.8 33.5 %copy-start.4 = (bf16[2,64,2304]{2,1,0:T(8,128)(2,1)S(1)}, bf16[2,64,2304]{2,1,0:T(8,128)(2,1)}, u32[]{:S(2)}) copy-start(bf16[2,64,2304]{2,1,0:T(8,128)(2,1)} %reduce-scatter.3.cloned.1.call-done) | copy-start | bytes 1769476
Sparse Core Ops, SparseCore 0:
  123.0 34.3 reduce-scatter.2
  162.6 32.5 all-gather.1
  215.0 31.9 reduce-scatter.4

commit v2 on v1

--- a/solution.py
+++ b/solution.py
@@ -18,6 +18,17 @@
     return (
         tensor * lax.rsqrt(jnp.mean(tensor * tensor, axis=-1, keepdims=True) + EPSILON) * scale_gain
     )
+
+
+def role(s):
+    x, z = s // 8, (s // 2) % 4
+    return 2 * ((x + z) % 4) + x % 2, 2 * (x // 2) + s % 2
+
+
+def device_of(slot, quarter):
+    x = 2 * (quarter // 2) + slot % 2
+    z = (slot // 2 - x + 4) % 4
+    return 8 * x + 2 * z + quarter % 2
 
 
 def attention_kernel(
@@ -51,9 +62,7 @@
     y = lax.axis_index("req")
     s = lax.axis_index("seq")
     core = s % 2
-    half = (s // 2) % 2
-    slot = s // 4
-    quarter = s % 4
+    slot, quarter = role(s)
     sibling = s + 1 - 2 * core
 
     def remote(src, dst, send, recv, to):
@@ -80,7 +89,7 @@
         pltpu.make_async_copy(cache_part(y, h), stage_part(y, h), ca_recv.at[y, h]).start()
 
     def fresh_copies(k, j, p, act):
-        target = 4 * (2 * y + j) + 2 * p + core
+        target = device_of(2 * y + j, 2 * p + core)
         own = (k == y) & (target == s)
         n = (k * 2 + j) * 2 + p
         for h in range(2):
@@ -102,7 +111,7 @@
                     pltpu.make_async_copy(src, dst, fd_recv.at[s, h]).start()
 
     def query_copies(k, j, act):
-        target = 4 * (2 * y + j) + quarter
+        target = device_of(2 * y + j, s % 4)
         own = (k == y) & (target == s)
         n = k * 2 + j
         src = q_ref.at[j, :, pl.ds(pl.multiple_of(k * 512, 512), 512)]
@@ -142,7 +151,7 @@
         order[i] = stage[slot_ref[i]]
 
     def cache_copies(i, p, act):
-        target = 4 * i + 2 * p + core
+        target = device_of(i, 2 * p + core)
         own = target == s
         src = order.at[i]
         dst = kvc.at[s]
@@ -331,7 +340,7 @@
     ordered = jnp.where(
         (page_table[:, 0, :] == 1)[:, :, None, None], kv_cache[:, 1:2], kv_cache[:, 0:1]
     ).reshape(req_dev, pages_dev * page_len, pair_width)
-    my_request = lax.dynamic_slice_in_dim(slot_request, my_seq // 4, 1)
+    my_request = lax.dynamic_slice_in_dim(slot_request, role(my_seq)[0], 1)
     my_len = jnp.sum(
         jnp.where(my_request == jnp.arange(cache_length.shape[0]), cache_length, 0)
     ).reshape(1)

time: 258 us -> 214 us (0.83)
  Pallas kernels: 105 us -> 64 us
    pallas_call x1, Pallas kernels: 105 us -> 64 us  [attention(): pl.pallas_call(attention_kernel, out_shape=jax.ShapeDtypeStruct((8, 64, 5...]
where the time goes in v2:
time: 214 us
  waiting for transfers between devices  97.2 us (45%)
  Pallas kernels  64 us (30%)
  matrix products  22.4 us (10%)
  between operations  13.2 us (6%)
  other arithmetic  11.6 us (5%)
  local copies, waits for them, and re-layouts  5.16 us (2%)
    pallas_call x1, Pallas kernels, attention(): pl.pallas_call(attention_kernel, out_shape=jax.ShapeDtypeStruct((8, 64, 5...  64 us
    all_gather x1, waiting for transfers between devices, body(): portion = lax.all_gather(normed, 'req', axis=0, tiled=True)  32.5 us
    reduce_scatter x1, waiting for transfers between devices, body(): lax.psum_scatter(partial_out.astype(jnp.bfloat16), 'req', scatter_dimensi...  32.5 us
    reduce_scatter x1, waiting for transfers between devices, body(): lax.psum_scatter(jnp.einsum('srf,fd->srd', hidden, w_down, preferred_elem...  32.2 us
    dot_general x1, matrix products, body(): jnp.einsum('srf,fd->srd', hidden, w_down, preferred_element_type=jnp.floa...  7.07 us
    dot_general x1, matrix products, body(): jnp.einsum('srd,df->srf', portion, w_gate, preferred_element_type=jnp.flo...  6.8 us
    dot_general x1, matrix products, body(): jnp.einsum('srd,df->srf', portion, w_up, preferred_element_type=jnp.float32)  5.76 us
  transfers between devices with their start and end apart: 3, of which 3 were waited for; matrix products, arithmetic and copies ran while one was open for 0% of the time, Pallas kernels for 0%

profile of v2, /device:TPU:1, one launch (start us, length us, event | category | flops | bytes accessed | tf_op | source)
XLA Modules:
  0.0 213.8 jit_solution(8868341465895303041)
XLA Ops:
  6.5 0.0 copy-start
  6.5 0.0 reduce-scatter.3.cloned.1.call-start
  6.5 0.8 broadcast_compare_fusion
  7.4 0.1 broadcast_in_dim.48
  7.5 0.1 broadcast_in_dim.49
  7.5 1.0 slice_bitcast_fusion.1
  8.5 1.2 dynamic_slice.3
  9.8 2.0 fusion.32
  11.7 0.1 bitcast_select_fusion.c_ref
  11.8 0.0 copy-start.1
  11.9 1.0 copy-done.1
  12.9 0.0 copy-start.2
  12.9 1.0 copy-done.2
  13.9 0.0 copy-start.3
  13.9 0.7 copy-done.3
  14.6 64.0 %attention.1 = bf16[8,64,512]{2,1,0:T(8,128)(2,1)S(1)} custom-call(s32[8]{0:T(128)S(1)} %copy-done.3, s32[1]{0:T(128)} %bitcast.1.len_ref, bf16[2,64,2048]{2,1,0:T(8,128)(2,1)S(1)} %copy-done.1, bf16[2,64,2048]{2,1,0:T(8,128)(2,1)S(1)} %copy-done.2, bf16[2,32,2048]{2,1,0:T(8,128)(2,1)S(1)} %bitcast_select_fusion.c_ref), custom_call_target="tpu_custom_call" | custom-call | tf_op jit(solution)/shard_map/attention/pallas_call | solution.py:281
  78.6 0.0 copy-done
  78.6 2.8 %convolution_convert_fusion = bf16[8,64,2304]{2,1,0:T(8,128)(2,1)} fusion(bf16[8,64,512]{2,1,0:T(8,128)(2,1)S(1)} %attention.1, bf16[512,2304]{1,0:T(8,128)(2,1)S(1)} %copy-done), kind=kOutput, calls=%fused_computation.7 | convolution fusion | flops 1209139200 | bytes 5242880 | tf_op jit(solution)/shard_map/srk,kd->srd/dot_general | solution.py:348
  81.4 0.0 copy-start.5
  81.4 0.0 copy-start.6
  81.4 0.0 copy-start.7
  81.4 0.0 reduce-scatter.3.cloned.1.call-update
  81.5 0.0 all-gather.2.cloned.1.call-start
  81.5 32.5 %reduce-scatter.3.cloned.1.call-done = bf16[2,64,2304]{2,1,0:T(8,128)(2,1)} async-done(((bf16[8,64,2304]{2,1,0:T(8,128)(2,1)}), bf16[2,64,2304]{2,1,0:T(8,128)(2,1)}) %reduce-scatter.3.cloned.1.call-update) | async-done | bytes 589840 | tf_op jit(solution)/shard_map/reduce_scatter | solution.py:349
  114.0 1.3 fusion.25
  115.3 0.0 copy-done.5
  115.3 0.0 copy-done.6
  115.3 1.5 multiply_reduce_fusion
  116.8 0.0 copy-done.7
  116.8 2.3 %multiply_convert_fusion = bf16[2,64,2304]{2,1,0:T(8,128)(2,1)} fusion(bf16[2,64,2304]{2,1,0:T(8,128)(2,1)} %reduce-scatter.3.cloned.1.call-done, bf16[2,64,2304]{2,1,0:T(8,128)(2,1)S(1)} %copy-done.5, f32[2304]{0:T(1024)S(1)} %copy-done.7, f32[2,64]{1,0:T(2,128)S(1)} %add_rsqrt_fusion.1, f32[2304]{0:T(1024)S(1)} %copy-done.6, f32[2,64]{1,0:T(2,128)S(1)} %add_rsqrt_fusion.2), kind=kLoop, calls=%fused_computation.30 | loop fusion | flops 2359296 | bytes 1788928 | tf_op jit(solution)/shard_map/convert_element_type | solution.py:353
  119.0 0.0 all-gather.2.cloned.1.call-update
  119.1 0.2 reduce-scatter.5.cloned.1.call-start
  119.3 32.5 %all-gather.2.cloned.1.call-done = bf16[8,64,2304]{2,1,0:T(8,128)(2,1)} async-done(((bf16[2,64,2304]{2,1,0:T(8,128)(2,1)}), bf16[8,64,2304]{2,1,0:T(8,128)(2,1)}) %all-gather.2.cloned.1.call-update) | async-done | bytes 2359312 | tf_op jit(solution)/shard_map/all_gather | solution.py:354
  151.8 0.0 copy-start.8
  151.8 6.8 %fusion.21 = f32[8,64,1152]{2,1,0:T(8,128)S(1)} fusion(bf16[8,64,2304]{2,1,0:T(8,128)(2,1)} %all-gather.2.cloned.1.call-done, bf16[2304,1152]{1,0:T(8,128)(2,1)} %param.22), kind=kOutput, calls=%fused_computation.17 | convolution fusion | flops 2722627584 | bytes 10027008 | tf_op jit(solution)/shard_map/srd,df->srf/dot_general | solution.py:355
  158.6 0.0 copy-done.8
  158.6 5.8 %fusion.12 = bf16[8,64,1152]{2,1,0:T(8,128)(2,1)S(1)} fusion(f32[8,64,1152]{2,1,0:T(8,128)S(1)} %fusion.21, bf16[8,64,2304]{2,1,0:T(8,128)(2,1)S(1)} %copy-done.8, bf16[2304,1152]{1,0:T(8,128)(2,1)} %param.23), kind=kOutput, calls=%fused_computation.10 | convolution fusion | flops 2719088640 | bytes 11206656 | tf_op jit(solution)/shard_map/srd,df->srf/dot_general | solution.py:356
  164.4 7.1 %fusion.6 = bf16[8,64,2304]{2,1,0:T(8,128)(2,1)} fusion(bf16[8,64,1152]{2,1,0:T(8,128)(2,1)S(1)} %fusion.12, bf16[1152,2304]{1,0:T(8,128)(2,1)} %param.24), kind=kOutput, calls=%fused_computation.6 | convolution fusion | flops 2719088640 | bytes 8847360 | tf_op jit(solution)/shard_map/srf,fd->srd/dot_general | solution.py:359
  171.4 0.0 copy-start.4
  171.4 0.0 reduce-scatter.5.cloned.1.call-update
  171.5 32.2 %reduce-scatter.5.cloned.1.call-done = bf16[2,64,2304]{2,1,0:T(8,128)(2,1)} async-done(((bf16[8,64,2304]{2,1,0:T(8,128)(2,1)}), bf16[2,64,2304]{2,1,0:T(8,128)(2,1)}) %reduce-scatter.5.cloned.1.call-update) | async-done | bytes 589840 | tf_op jit(solution)/shard_map/reduce_scatter | solution.py:358
  203.6 1.3 fusion.28
  204.9 0.0 copy-done.4
  204.9 2.4 %fusion.31 = bf16[2,64,2304]{2,1,0:T(8,128)(2,1)} fusion(bf16[2,64,2304]{2,1,0:T(8,128)(2,1)} %reduce-scatter.5.cloned.1.call-done, bf16[2,64,2304]{2,1,0:T(8,128)(2,1)S(1)} %copy-done.4, bf16[2,64,2304]{2,1,0:T(8,128)(2,1)S(1)} %copy-done.5, f32[2304]{0:T(1024)} %param.27, f32[2,64]{1,0:T(2,128)S(1)} %add_rsqrt_fusion, f32[2304]{0:T(1024)S(1)} %copy-done.6, ...), kind=kLoop, calls=%fused_computation.29 | loop fusion | flops 2949120 | bytes 2378752 | tf_op jit(solution)/shard_map/convert_element_type | solution.py:366
  (4 shorter events, 0.0 us)
Async XLA Ops:
  6.5 72.1 %copy-start = (bf16[512,2304]{1,0:T(8,128)(2,1)S(1)}, bf16[512,2304]{1,0:T(8,128)(2,1)}, u32[]{:S(2)}) copy-start(bf16[512,2304]{1,0:T(8,128)(2,1)} %param.21) | copy-start | bytes 7077892
  6.5 107.4 %reduce-scatter.3.cloned.1.call-start = ((), (), s32[]{:S(2)}) async-start(), calls=%async_computation.2 | async-start | bytes 2949120 | tf_op jit(solution)/shard_map/reduce_scatter | solution.py:349
  11.8 1.0 copy-start.1
  12.9 1.0 copy-start.2
  13.9 0.7 copy-start.3
  81.4 33.8 %copy-start.5 = (bf16[2,64,2304]{2,1,0:T(8,128)(2,1)S(1)}, bf16[2,64,2304]{2,1,0:T(8,128)(2,1)}, u32[]{:S(2)}) copy-start(bf16[2,64,2304]{2,1,0:T(8,128)(2,1)} %param.16) | copy-start | bytes 1769476
  81.4 33.8 %copy-start.6 = (f32[2304]{0:T(1024)S(1)}, f32[2304]{0:T(1024)}, u32[]{:S(2)}) copy-start(f32[2304]{0:T(1024)} %param.25) | copy-start | bytes 27652
  81.4 35.3 %copy-start.7 = (f32[2304]{0:T(1024)S(1)}, f32[2304]{0:T(1024)}, u32[]{:S(2)}) copy-start(f32[2304]{0:T(1024)} %param.26) | copy-start | bytes 27652
  81.5 70.3 %all-gather.2.cloned.1.call-start = ((), (), s32[]{:S(2)}) async-start(), calls=%async_computation.3 | async-start | bytes 2949120 | tf_op jit(solution)/shard_map/all_gather | solution.py:354
  119.1 84.6 %reduce-scatter.5.cloned.1.call-start = ((), (), s32[]{:S(2)}) async-start(), calls=%async_computation.4 | async-start | bytes 2949120 | tf_op jit(solution)/shard_map/reduce_scatter | solution.py:358
  151.8 6.8 %copy-start.8 = (bf16[8,64,2304]{2,1,0:T(8,128)(2,1)S(1)}, bf16[8,64,2304]{2,1,0:T(8,128)(2,1)}, u32[]{:S(2)}) copy-start(bf16[8,64,2304]{2,1,0:T(8,128)(2,1)} %all-gather.2.cloned.1.call-done) | copy-start | bytes 7077892
  171.4 33.5 %copy-start.4 = (bf16[2,64,2304]{2,1,0:T(8,128)(2,1)S(1)}, bf16[2,64,2304]{2,1,0:T(8,128)(2,1)}, u32[]{:S(2)}) copy-start(bf16[2,64,2304]{2,1,0:T(8,128)(2,1)} %reduce-scatter.3.cloned.1.call-done) | copy-start | bytes 1769476
Sparse Core Ops, SparseCore 0:
  81.6 32.3 reduce-scatter.2
  119.2 32.5 all-gather.1
  171.6 31.9 reduce-scatter.4

commit v3 on v2

--- a/solution.py
+++ b/solution.py
@@ -318,6 +318,231 @@
     )(slot_request, length, query, fresh, cache)
 
 
+def ffn_kernel(
+    att_ref,
+    res_ref,
+    wo_hbm,
+    wg_hbm,
+    wu_hbm,
+    wd_hbm,
+    ga_ref,
+    gp_ref,
+    gq_ref,
+    out_ref,
+    wo,
+    wg,
+    wu,
+    wd,
+    parts,
+    passed,
+    relay,
+    arrived,
+    gathered,
+    state,
+    hidden,
+    w_sem,
+    rs_send,
+    rs_recv,
+    ag_send,
+    ag_recv,
+):
+    y = lax.axis_index("req")
+    s = lax.axis_index("seq")
+    up, down = (y + 1) % 4, (y + 3) % 4
+    loads = [
+        pltpu.make_async_copy(src, dst, w_sem.at[n])
+        for n, (src, dst) in enumerate(((wo_hbm, wo), (wg_hbm, wg), (wu_hbm, wu), (wd_hbm, wd)))
+    ]
+    for cp in loads:
+        cp.start()
+    barrier = pltpu.get_barrier_semaphore()
+    for to in (up, down):
+        pl.semaphore_signal(barrier, inc=1, device_id=(to, s), device_id_type=MESH)
+    pl.semaphore_wait(barrier, 2)
+
+    halves = (pl.ds(0, 32), pl.ds(32, 32))
+
+    def remote(src, dst, send, recv, to):
+        return pltpu.make_async_remote_copy(
+            src_ref=src,
+            dst_ref=dst,
+            send_sem=send,
+            recv_sem=recv,
+            device_id=(to, s),
+            device_id_type=MESH,
+        )
+
+    def await_copy(dst, sem):
+        pltpu.make_async_copy(dst, dst, sem).wait()
+
+    def first_copies(e, b):
+        send, recv = rs_send.at[e, b], rs_recv.at[e, b]
+        mine = parts.at[e, b]
+        return (
+            remote(mine.at[2, halves[0]], relay.at[e, b, 0], send.at[0], recv.at[0], up),
+            remote(mine.at[2, halves[1]], relay.at[e, b, 1], send.at[1], recv.at[1], down),
+            remote(
+                mine.at[1, halves[1]], arrived.at[e, b, 0, halves[1]], send.at[2], recv.at[2], up
+            ),
+            remote(
+                mine.at[3, halves[0]], arrived.at[e, b, 1, halves[0]], send.at[3], recv.at[3], down
+            ),
+        )
+
+    def relay_copy(e, b, d):
+        dst = arrived.at[e, b, d, halves[d]]
+        send, recv = rs_send.at[e, b, 4 + d], rs_recv.at[e, b, 4 + d]
+        return remote(passed.at[e, b, d], dst, send, recv, (up, down)[d])
+
+    def start_sum(e, b):
+        for cp in first_copies(e, b):
+            cp.start()
+
+    def relay_sum(e, b):
+        for d in range(2):
+            await_copy(relay.at[e, b, d], rs_recv.at[e, b, d])
+            mine = parts[e, b, 1 + 2 * d, 32 * d : 32 * d + 32]
+            passed[e, b, d] = (
+                relay[e, b, d].astype(jnp.float32) + mine.astype(jnp.float32)
+            ).astype(jnp.bfloat16)
+            relay_copy(e, b, d).start()
+
+    def finish_sum(e, b):
+        await_copy(arrived.at[e, b, 0, halves[1]], rs_recv.at[e, b, 2])
+        await_copy(arrived.at[e, b, 1, halves[0]], rs_recv.at[e, b, 3])
+        await_copy(arrived.at[e, b, 0, halves[0]], rs_recv.at[e, b, 4])
+        await_copy(arrived.at[e, b, 1, halves[1]], rs_recv.at[e, b, 5])
+        return (
+            parts[e, b, 0].astype(jnp.float32)
+            + arrived[e, b, 0].astype(jnp.float32)
+            + arrived[e, b, 1].astype(jnp.float32)
+        )
+
+    def spread_copies(b):
+        send, recv = ag_send.at[b], ag_recv.at[b]
+        mine = gathered.at[b, 0]
+        return (
+            remote(mine, gathered.at[b, 3], send.at[0], recv.at[0], up),
+            remote(mine, gathered.at[b, 1], send.at[1], recv.at[1], down),
+        )
+
+    def onward_copy(b, d):
+        src = gathered.at[b, 3 - 2 * d, halves[d]]
+        dst = gathered.at[b, 2, halves[d]]
+        send, recv = ag_send.at[b, 2 + d], ag_recv.at[b, 2 + d]
+        return remote(src, dst, send, recv, (up, down)[d])
+
+    def onward(b):
+        for d in range(2):
+            await_copy(gathered.at[b, 3 - 2 * d], ag_recv.at[b, d])
+            onward_copy(b, d).start()
+
+    def project(b):
+        rows = jnp.concatenate([att_ref[2 * ((y + r) % 4) + b] for r in range(4)], axis=0)
+        product = jnp.dot(rows, wo[...], preferred_element_type=jnp.float32)
+        parts[0, b] = product.astype(jnp.bfloat16).reshape(4, 64, 2304)
+
+    def middle(b):
+        level = res_ref[b].astype(jnp.float32) + rms_scale(finish_sum(0, b), ga_ref[...])
+        state[b] = level
+        gathered[b, 0] = rms_scale(level, gp_ref[...]).astype(jnp.bfloat16)
+        for cp in spread_copies(b):
+            cp.start()
+
+    def widen(b):
+        for d in range(2):
+            await_copy(gathered.at[b, 2, halves[d]], ag_recv.at[b, 2 + d])
+        rows = gathered[b].reshape(256, 2304)
+        gate = jnp.dot(rows, wg[...], preferred_element_type=jnp.float32)
+        lift = jnp.dot(rows, wu[...], preferred_element_type=jnp.float32)
+        hidden[...] = (jax.nn.gelu(gate, approximate=True) * lift).astype(jnp.bfloat16)
+
+    def narrow(b):
+        product = jnp.dot(hidden[...], wd[...], preferred_element_type=jnp.float32)
+        parts[1, b] = product.astype(jnp.bfloat16).reshape(4, 64, 2304)
+        start_sum(1, b)
+
+    def last(b):
+        out_ref[b] = (state[b] + rms_scale(finish_sum(1, b), gq_ref[...])).astype(jnp.bfloat16)
+
+    loads[0].wait()
+    project(0)
+    start_sum(0, 0)
+    project(1)
+    relay_sum(0, 0)
+    start_sum(0, 1)
+    middle(0)
+    relay_sum(0, 1)
+    onward(0)
+    middle(1)
+    for cp in loads[1:]:
+        cp.wait()
+    widen(0)
+    onward(1)
+    narrow(0)
+    widen(1)
+    relay_sum(1, 0)
+    narrow(1)
+    last(0)
+    relay_sum(1, 1)
+    last(1)
+    for b in range(2):
+        for e in range(2):
+            for cp in first_copies(e, b):
+                cp.wait_send()
+        for cp in spread_copies(b):
+            cp.wait_send()
+        for d in range(2):
+            relay_copy(0, b, d).wait_send()
+            relay_copy(1, b, d).wait_send()
+            onward_copy(b, d).wait_send()
+
+
+def feed_forward(attended, residual, w_out, w_gate, w_up, w_down, gain_attn, gain_pre, gain_post):
+    dma = pltpu.SemaphoreType.DMA
+    vmem = pl.BlockSpec(memory_space=pltpu.VMEM)
+    hbm = pl.BlockSpec(memory_space=pl.ANY)
+    bf16 = jnp.bfloat16
+    return pl.pallas_call(
+        ffn_kernel,
+        out_shape=jax.ShapeDtypeStruct((2, 64, 2304), bf16),
+        in_specs=[vmem, vmem, hbm, hbm, hbm, hbm, vmem, vmem, vmem],
+        out_specs=vmem,
+        scratch_shapes=[
+            pltpu.VMEM(w_out.shape, bf16),
+            pltpu.VMEM(w_gate.shape, bf16),
+            pltpu.VMEM(w_up.shape, bf16),
+            pltpu.VMEM(w_down.shape, bf16),
+            pltpu.VMEM((2, 2, 4, 64, 2304), bf16),
+            pltpu.VMEM((2, 2, 2, 32, 2304), bf16),
+            pltpu.VMEM((2, 2, 2, 32, 2304), bf16),
+            pltpu.VMEM((2, 2, 2, 64, 2304), bf16),
+            pltpu.VMEM((2, 4, 64, 2304), bf16),
+            pltpu.VMEM((2, 64, 2304), jnp.float32),
+            pltpu.VMEM((256, 1152), bf16),
+            dma((4,)),
+            dma((2, 2, 6)),
+            dma((2, 2, 6)),
+            dma((2, 4)),
+            dma((2, 4)),
+        ],
+        compiler_params=pltpu.CompilerParams(
+            collective_id=1, has_side_effects=True, vmem_limit_bytes=52 * 1024 * 1024
+        ),
+        name="feed_forward",
+    )(
+        attended,
+        residual,
+        w_out,
+        w_gate,
+        w_up,
+        w_down,
+        gain_attn.reshape(1, -1),
+        gain_pre.reshape(1, -1),
+        gain_post.reshape(1, -1),
+    )
+
+
 def body(
     query,
     fresh_kv,
@@ -345,25 +570,9 @@
         jnp.where(my_request == jnp.arange(cache_length.shape[0]), cache_length, 0)
     ).reshape(1)
     attended = attention(slot_request, my_len, query, fresh_kv, ordered)
-    partial_out = jnp.einsum("srk,kd->srd", attended, w_out, preferred_element_type=jnp.float32)
-    mixed = lax.psum_scatter(
-        partial_out.astype(jnp.bfloat16), "req", scatter_dimension=0, tiled=True
-    ).astype(jnp.float32)
-    layer_state = residual.astype(jnp.float32) + rms_scale(mixed, gain_attn)
-    normed = rms_scale(layer_state, gain_pre).astype(jnp.bfloat16)
-    portion = lax.all_gather(normed, "req", axis=0, tiled=True)
-    gate_proj = jnp.einsum("srd,df->srf", portion, w_gate, preferred_element_type=jnp.float32)
-    up_proj = jnp.einsum("srd,df->srf", portion, w_up, preferred_element_type=jnp.float32)
-    hidden = (jax.nn.gelu(gate_proj, approximate=True) * up_proj).astype(jnp.bfloat16)
-    mlp_out = lax.psum_scatter(
-        jnp.einsum("srf,fd->srd", hidden, w_down, preferred_element_type=jnp.float32).astype(
-            jnp.bfloat16
-        ),
-        "req",
-        scatter_dimension=0,
-        tiled=True,
-    ).astype(jnp.float32)
-    return (layer_state + rms_scale(mlp_out, gain_post)).astype(jnp.bfloat16)
+    return feed_forward(
+        attended, residual, w_out, w_gate, w_up, w_down, gain_attn, gain_pre, gain_post
+    )
 
 
 def solution(mesh):

time: 214 us -> 140 us (0.65)
  waiting for transfers between devices: 97.2 us -> 0 us
  Pallas kernels: 64 us -> 126 us
  matrix products: 22.4 us -> 0 us
  between operations: 13.2 us -> 0.05 us
  other arithmetic: 11.6 us -> 2.77 us
  local copies, waits for them, and re-layouts: 5.16 us -> 9.14 us
    reduce_scatter x2 -> x0, waiting for transfers between devices: 64.6 us -> none  [the longest x1 32.5 us: body(): lax.psum_scatter(partial_out.astype(jnp.bfloat16), 'req', scatter_dimensi...]
    pallas_call x0 -> x1, Pallas kernels: none -> 61.7 us  [feed_forward(): pl.pallas_call(ffn_kernel, out_shape=jax.ShapeDtypeStruct((2, 64, 2304),...]
    all_gather x1 -> x0, waiting for transfers between devices: 32.5 us -> none  [body(): portion = lax.all_gather(normed, 'req', axis=0, tiled=True)]
    dot_general x4 -> x0, matrix products: 22.4 us -> none  [the longest x1 7.07 us: body(): jnp.einsum('srf,fd->srd', hidden, w_down, preferred_element_type=jnp.floa...]
    convert_element_type x2 -> x0, other arithmetic: 4.66 us -> none  [the longest x1 2.4 us: body(): return (layer_state + rms_scale(mlp_out, gain_post)).astype(jnp.bfloat16)]
    reduce_sum x3 -> x0, other arithmetic: 4.02 us -> none  [rms_scale(): jnp.mean(tensor * tensor, axis=-1, keepdims=True) + EPSILON]
    reshape x0 -> x3, local copies, waits for them, and re-layouts: none -> 2.14 us  [the longest x1 0.71 us: feed_forward(): gain_attn.reshape(1, -1)]
    unnamed x19 -> x10, local copies, waits for them, and re-layouts: 2.76 us -> 4.62 us
  transfers between devices with their start and end apart: 3 -> 0, of which waited for: 3 -> 0; matrix products, arithmetic and copies ran while one was open for 0% -> 0% of each run, Pallas kernels for 0% -> 0%
where the time goes in v3:
time: 140 us; the launch traced here: 138 us
  Pallas kernels  126 us (90%)
  local copies, waits for them, and re-layouts  9.14 us (7%)
  other arithmetic  2.77 us (2%)
    pallas_call x1, Pallas kernels, attention(): pl.pallas_call(attention_kernel, out_shape=jax.ShapeDtypeStruct((8, 64, 5...  64 us
    pallas_call x1, Pallas kernels, feed_forward(): pl.pallas_call(ffn_kernel, out_shape=jax.ShapeDtypeStruct((2, 64, 2304),...  61.7 us
    unnamed x10, local copies, waits for them, and re-layouts  4.62 us

profile of v3, /device:TPU:1, one launch (start us, length us, event | category | flops | bytes accessed | tf_op | source)
XLA Modules:
  0.0 137.7 jit_solution(7459243144388040620)
XLA Ops:
  0.0 1.2 dynamic_slice.3
  1.2 2.0 %fusion = s32[]{:T(128)} fusion(s32[8]{0:T(128)} %param.19, s32[]{:T(128)} %bitcast), kind=kLoop, calls=%fused_computation.5 | loop fusion | flops 23 | bytes 40 | tf_op jit(solution)/shard_map/reduce_sum | solution.py:569
  3.2 0.7 broadcast_compare_fusion
  3.9 0.1 broadcast_in_dim.42
  4.0 0.1 broadcast_in_dim.43
  4.1 0.7 reshape.24.ga_ref
  4.8 0.7 reshape.25.gp_ref
  5.5 0.7 reshape.26.gq_ref
  6.2 1.0 slice_bitcast_fusion.1
  7.2 0.1 bitcast_select_fusion.c_ref
  7.3 0.0 copy-start.1
  7.3 1.0 copy-done.1
  8.4 0.0 copy-start.2
  8.4 1.0 copy-done.2
  9.4 0.0 copy-start.3
  9.4 0.7 copy-done.3
  10.1 64.0 %attention.1.att_ref = bf16[8,64,512]{2,1,0:T(8,128)(2,1)S(1)} custom-call(s32[8]{0:T(128)S(1)} %copy-done.3, s32[1]{0:T(128)} %bitcast.1.len_ref, bf16[2,64,2048]{2,1,0:T(8,128)(2,1)S(1)} %copy-done.1, bf16[2,64,2048]{2,1,0:T(8,128)(2,1)S(1)} %copy-done.2, bf16[2,32,2048]{2,1,0:T(8,128)(2,1)S(1)} %bitcast_select_fusion.c_ref), custom_call_target="tpu_custom_call" | custom-call | tf_op jit(solution)/shard_map/attention/pallas_call | solution.py:281
  74.1 0.0 copy-start
  74.1 1.1 copy-done
  75.2 61.7 %feed_forward.1 = bf16[2,64,2304]{2,1,0:T(8,128)(2,1)S(1)} custom-call(bf16[8,64,512]{2,1,0:T(8,128)(2,1)S(1)} %attention.1.att_ref, bf16[2,64,2304]{2,1,0:T(8,128)(2,1)S(1)} %copy-done, bf16[512,2304]{1,0:T(8,128)(2,1)} %wo_hbm.1, bf16[2304,1152]{1,0:T(8,128)(2,1)} %wg_hbm.1, bf16[2304,1152]{1,0:T(8,128)(2,1)} %wu_hbm.1, bf16[1152,2304]{1,0:T(8,128)(2,1)} %wd_hbm.1, ...), custom_call_target="tpu_custom_call" | custom-call | tf_op jit(solution)/shard_map/feed_forward/pallas_call | solution.py:506
  136.9 0.8 copy.19
  (1 shorter events, 0.0 us)
Async XLA Ops:
  7.3 1.0 copy-start.1
  8.4 1.0 copy-start.2
  9.4 0.7 copy-start.3
  74.1 1.1 copy-start

commit v4 on v3

--- a/solution.py
+++ b/solution.py
@@ -12,6 +12,7 @@
 EPSILON = 1e-06
 LOG2E = 1.4426950408889634
 MESH = pl.DeviceIdType.MESH
+VMEM_LIMIT = 67043328
 
 
 def rms_scale(tensor, scale_gain):
@@ -32,12 +33,18 @@
 
 
 def attention_kernel(
+    slot_hbm,
+    len_hbm,
+    page_hbm,
+    q_ref,
+    f_ref,
+    pages_hbm,
+    att_ref,
     slot_ref,
     len_ref,
-    q_ref,
-    f_ref,
+    page_ref,
+    pages_ref,
     c_ref,
-    att_ref,
     qbuf,
     kvf,
     kvc,
@@ -46,6 +53,7 @@
     obuf,
     acc,
     den,
+    in_sem,
     ca_send,
     ca_recv,
     q_send,
@@ -73,6 +81,45 @@
     def lanes(start):
         return pl.ds(pl.multiple_of(start, 256), 256)
 
+    loads = [
+        pltpu.make_async_copy(src, dst, in_sem.at[n])
+        for n, (src, dst) in enumerate(
+            (
+                (pages_hbm, pages_ref),
+                (page_hbm, page_ref),
+                (slot_hbm, slot_ref),
+                (len_hbm, len_ref),
+            )
+        )
+    ]
+    for cp in loads:
+        cp.start()
+
+    barrier = pltpu.get_barrier_semaphore()
+
+    def greet(*to):
+        pl.semaphore_signal(barrier, inc=1, device_id=to, device_id_type=MESH)
+
+    home = slot // 2
+    for d in range(1, 16):
+        greet(y, (s + 2 * d) % 32)
+    for d in range(1, 4):
+        greet((y + d) % 4, s)
+    greet(y, sibling)
+
+    @pl.when(home != y)
+    def _():
+        for n in range(16):
+            greet(home, 2 * n + core)
+
+    for cp in loads:
+        cp.wait()
+    for r in range(2):
+        for j in range(2):
+            c_ref[r, 16 * j : 16 * j + 16] = pages_ref[r, page_ref[r, 0, j]]
+
+    pl.semaphore_wait(barrier, 15 + 3 + 1 + 12)
+
     def cache_part(k, h):
         return c_ref.at[:, :, lanes(h * 1024 + k * 256)]
 
@@ -191,7 +238,7 @@
         pltpu.make_async_copy(kvf.at[src], kvf.at[src], f_recv.at[j]).wait()
         pltpu.make_async_copy(kvc.at[src], kvc.at[src], c_recv.at[src]).wait()
 
-    length = len_ref[0]
+    length = len_ref[slot_ref[slot]]
     for n in range(12):
         fresh = n - 4
         if n < 4:
@@ -276,20 +323,19 @@
         result_copies(j, "wait")
 
 
-def attention(slot_request, length, query, fresh, cache):
+def attention(slot_request, cache_length, page_table, query, fresh, cache):
     dma = pltpu.SemaphoreType.DMA
     return pl.pallas_call(
         attention_kernel,
         out_shape=jax.ShapeDtypeStruct((8, 64, 512), jnp.bfloat16),
-        in_specs=[
-            pl.BlockSpec(memory_space=pltpu.SMEM),
-            pl.BlockSpec(memory_space=pltpu.SMEM),
-            pl.BlockSpec(memory_space=pltpu.VMEM),
-            pl.BlockSpec(memory_space=pltpu.VMEM),
-            pl.BlockSpec(memory_space=pltpu.VMEM),
-        ],
+        in_specs=[pl.BlockSpec(memory_space=pltpu.HBM)] * 6,
         out_specs=pl.BlockSpec(memory_space=pltpu.VMEM),
         scratch_shapes=[
+            pltpu.SMEM((8,), jnp.int32),
+            pltpu.SMEM((8,), jnp.int32),
+            pltpu.SMEM((2, 1, 2), jnp.int32),
+            pltpu.VMEM((2, 2, 16, 2048), jnp.bfloat16),
+            pltpu.VMEM((2, 32, 2048), jnp.bfloat16),
             pltpu.VMEM((8, 64, 512), jnp.bfloat16),
             pltpu.VMEM((32, 64, 512), jnp.bfloat16),
             pltpu.VMEM((32, 32, 512), jnp.bfloat16),
@@ -298,6 +344,7 @@
             pltpu.VMEM((8, 64, 512), jnp.bfloat16),
             pltpu.VMEM((2, 512, 256), jnp.float32),
             pltpu.VMEM((2, 512, 128), jnp.float32),
+            dma((4,)),
             dma((4, 2)),
             dma((4, 2)),
             dma((8,)),
@@ -312,23 +359,27 @@
             dma((8,)),
         ],
         compiler_params=pltpu.CompilerParams(
-            has_side_effects=True, vmem_limit_bytes=40 * 1024 * 1024
+            collective_id=0, has_side_effects=True, vmem_limit_bytes=VMEM_LIMIT
         ),
         name="attention",
-    )(slot_request, length, query, fresh, cache)
+    )(slot_request, cache_length, page_table, query, fresh, cache)
 
 
 def ffn_kernel(
     att_ref,
-    res_ref,
+    res_hbm,
     wo_hbm,
     wg_hbm,
     wu_hbm,
     wd_hbm,
+    ga_hbm,
+    gp_hbm,
+    gq_hbm,
+    out_ref,
     ga_ref,
     gp_ref,
     gq_ref,
-    out_ref,
+    res_ref,
     wo,
     wg,
     wu,
@@ -351,7 +402,18 @@
     up, down = (y + 1) % 4, (y + 3) % 4
     loads = [
         pltpu.make_async_copy(src, dst, w_sem.at[n])
-        for n, (src, dst) in enumerate(((wo_hbm, wo), (wg_hbm, wg), (wu_hbm, wu), (wd_hbm, wd)))
+        for n, (src, dst) in enumerate(
+            (
+                (wo_hbm, wo),
+                (res_hbm, res_ref),
+                (ga_hbm, ga_ref),
+                (gp_hbm, gp_ref),
+                (gq_hbm, gq_ref),
+                (wg_hbm, wg),
+                (wu_hbm, wu),
+                (wd_hbm, wd),
+            )
+        )
     ]
     for cp in loads:
         cp.start()
@@ -443,9 +505,9 @@
         parts[0, b] = product.astype(jnp.bfloat16).reshape(4, 64, 2304)
 
     def middle(b):
-        level = res_ref[b].astype(jnp.float32) + rms_scale(finish_sum(0, b), ga_ref[...])
+        level = res_ref[b].astype(jnp.float32) + rms_scale(finish_sum(0, b), ga_ref[...][None, :])
         state[b] = level
-        gathered[b, 0] = rms_scale(level, gp_ref[...]).astype(jnp.bfloat16)
+        gathered[b, 0] = rms_scale(level, gp_ref[...][None, :]).astype(jnp.bfloat16)
         for cp in spread_copies(b):
             cp.start()
 
@@ -463,7 +525,7 @@
         start_sum(1, b)
 
     def last(b):
-        out_ref[b] = (state[b] + rms_scale(finish_sum(1, b), gq_ref[...])).astype(jnp.bfloat16)
+        out_ref[b] = (state[b] + rms_scale(finish_sum(1, b), gq_ref[...][None, :])).astype(jnp.bfloat16)
 
     loads[0].wait()
     project(0)
@@ -471,11 +533,13 @@
     project(1)
     relay_sum(0, 0)
     start_sum(0, 1)
+    for cp in loads[1:5]:
+        cp.wait()
     middle(0)
     relay_sum(0, 1)
     onward(0)
     middle(1)
-    for cp in loads[1:]:
+    for cp in loads[5:]:
         cp.wait()
     widen(0)
     onward(1)
@@ -501,14 +565,18 @@
 def feed_forward(attended, residual, w_out, w_gate, w_up, w_down, gain_attn, gain_pre, gain_post):
     dma = pltpu.SemaphoreType.DMA
     vmem = pl.BlockSpec(memory_space=pltpu.VMEM)
-    hbm = pl.BlockSpec(memory_space=pl.ANY)
+    hbm = pl.BlockSpec(memory_space=pltpu.HBM)
     bf16 = jnp.bfloat16
     return pl.pallas_call(
         ffn_kernel,
         out_shape=jax.ShapeDtypeStruct((2, 64, 2304), bf16),
-        in_specs=[vmem, vmem, hbm, hbm, hbm, hbm, vmem, vmem, vmem],
+        in_specs=[vmem] + [hbm] * 8,
         out_specs=vmem,
         scratch_shapes=[
+            pltpu.VMEM(gain_attn.shape, jnp.float32),
+            pltpu.VMEM(gain_attn.shape, jnp.float32),
+            pltpu.VMEM(gain_attn.shape, jnp.float32),
+            pltpu.VMEM(residual.shape, bf16),
             pltpu.VMEM(w_out.shape, bf16),
             pltpu.VMEM(w_gate.shape, bf16),
             pltpu.VMEM(w_up.shape, bf16),
@@ -520,14 +588,14 @@
             pltpu.VMEM((2, 4, 64, 2304), bf16),
             pltpu.VMEM((2, 64, 2304), jnp.float32),
             pltpu.VMEM((256, 1152), bf16),
-            dma((4,)),
+            dma((8,)),
             dma((2, 2, 6)),
             dma((2, 2, 6)),
             dma((2, 4)),
             dma((2, 4)),
         ],
         compiler_params=pltpu.CompilerParams(
-            collective_id=1, has_side_effects=True, vmem_limit_bytes=52 * 1024 * 1024
+            collective_id=1, has_side_effects=True, vmem_limit_bytes=VMEM_LIMIT
         ),
         name="feed_forward",
     )(
@@ -537,9 +605,9 @@
         w_gate,
         w_up,
         w_down,
-        gain_attn.reshape(1, -1),
-        gain_pre.reshape(1, -1),
-        gain_post.reshape(1, -1),
+        gain_attn,
+        gain_pre,
+        gain_post,
     )
 
 
@@ -559,17 +627,9 @@
     gain_pre,
     gain_post,
 ):
-    req_dev, row_count = (query.shape[0], query.shape[1])
-    pages_dev, page_len, pair_width = kv_cache.shape[1:]
-    my_seq = lax.axis_index("seq")
-    ordered = jnp.where(
-        (page_table[:, 0, :] == 1)[:, :, None, None], kv_cache[:, 1:2], kv_cache[:, 0:1]
-    ).reshape(req_dev, pages_dev * page_len, pair_width)
-    my_request = lax.dynamic_slice_in_dim(slot_request, role(my_seq)[0], 1)
-    my_len = jnp.sum(
-        jnp.where(my_request == jnp.arange(cache_length.shape[0]), cache_length, 0)
-    ).reshape(1)
-    attended = attention(slot_request, my_len, query, fresh_kv, ordered)
+    attended = attention(
+        slot_request, cache_length, page_table, query, fresh_kv, kv_cache
+    )
     return feed_forward(
         attended, residual, w_out, w_gate, w_up, w_down, gain_attn, gain_pre, gain_post
     )

time: 140 us -> 128 us (0.914); the launches traced: 138 us -> 128 us
  local copies, waits for them, and re-layouts: 9.14 us -> 1.92 us
  other arithmetic: 2.77 us -> 0 us
    pallas_call x1, Pallas kernels: 64 us -> 58.6 us  [attention(): pl.pallas_call(attention_kernel, out_shape=jax.ShapeDtypeStruct((8, 64, 5...]
    pallas_call x1, Pallas kernels: 61.7 us -> 67.1 us  [feed_forward(): pl.pallas_call(ffn_kernel, out_shape=jax.ShapeDtypeStruct((2, 64, 2304),...]
    unnamed x10 -> x1, local copies, waits for them, and re-layouts: 4.62 us -> 1.92 us
    reshape x3 -> x0, local copies, waits for them, and re-layouts: 2.14 us -> none  [the longest x1 0.71 us: feed_forward(): gain_attn.reshape(1, -1)]
    reduce_sum x1 -> x0, other arithmetic: 2 us -> none  [body(): jnp.sum(jnp.where(my_request == jnp.arange(cache_length.shape[0]), cache_...]
where the time goes in v4:
time: 128 us
  Pallas kernels  126 us (98%)
  local copies, waits for them, and re-layouts  1.92 us (2%)
    pallas_call x1, Pallas kernels, feed_forward(): pl.pallas_call(ffn_kernel, out_shape=jax.ShapeDtypeStruct((2, 64, 2304),...  67.1 us
    pallas_call x1, Pallas kernels, attention(): pl.pallas_call(attention_kernel, out_shape=jax.ShapeDtypeStruct((8, 64, 5...  58.6 us

profile of v4, /device:TPU:1, one launch (start us, length us, event | category | flops | bytes accessed | tf_op | source)
XLA Modules:
  0.0 127.6 jit_solution(6225243494996108350)
XLA Ops:
  0.0 58.6 %attention.1.att_ref = bf16[8,64,512]{2,1,0:T(8,128)(2,1)} custom-call(s32[8]{0:T(128)} %slot_hbm.1, s32[8]{0:T(128)} %len_hbm.1, s32[2,1,2]{2,1,0:T(1,128)} %page_hbm.1, bf16[2,64,2048]{2,1,0:T(8,128)(2,1)} %q_ref.1, bf16[2,64,2048]{2,1,0:T(8,128)(2,1)} %f_ref.1, bf16[2,2,16,2048]{3,2,1,0:T(8,128)(2,1)} %pages_hbm.1), custom_call_target="tpu_custom_call" | custom-call | tf_op jit(solution)/shard_map/attention/pallas_call | solution.py:328
  58.6 67.1 %feed_forward.1 = bf16[2,64,2304]{2,1,0:T(8,128)(2,1)} custom-call(bf16[8,64,512]{2,1,0:T(8,128)(2,1)} %attention.1.att_ref, bf16[2,64,2304]{2,1,0:T(8,128)(2,1)} %res_hbm.1, bf16[512,2304]{1,0:T(8,128)(2,1)} %wo_hbm.1, bf16[2304,1152]{1,0:T(8,128)(2,1)} %wg_hbm.1, bf16[2304,1152]{1,0:T(8,128)(2,1)} %wu_hbm.1, bf16[1152,2304]{1,0:T(8,128)(2,1)} %wd_hbm.1, ...), custom_call_target="tpu_custom_call" | custom-call | tf_op jit(solution)/shard_map/feed_forward/pallas_call | solution.py:570
  125.7 1.9 %copy.16 = bf16[2,64,2304]{2,1,0:T(8,128)(2,1)} copy(bf16[2,64,2304]{2,1,0:T(8,128)(2,1)} %feed_forward.1) | data formatting | bytes 1179648
